TPU v7x, 512 devices: a whole 4x8x8 slice. The times are simulated.
512 devices in a mesh: interval: 8 (over y), seq: 8 (over x, core), head: 8 (over z).
Axes of the slice: x: 4, y: 8, z: 8, core: 2. Of those that a mesh axis runs over, the one named last changes fastest.
Arguments:
- hidden_in: bfloat16 [8, 2048, 1536], P('interval', 'seq'), may hold values from -6 to 6
- ctx_grad: bfloat16 [8, 2048, 1536], P('interval', 'seq', 'head'), may hold values from -6 to 6
- w_query: bfloat16 [1536, 1536], P('head'), may hold values from -0.15625 to 0.15625
- w_key: bfloat16 [1536, 1536], P('head'), may hold values from -0.15625 to 0.15625
- w_value: bfloat16 [1536, 1536], P('head'), may hold values from -0.15625 to 0.15625
- w_junction: bfloat16 [1536, 128], replicated, may hold values from -0.15625 to 0.15625
- donor_pos: int32 [8, 8, 8, 64], P('interval', 'seq', None, 'head'), may hold values from 0 to 255
- acceptor_pos: int32 [8, 8, 8, 64], P('interval', 'seq', None, 'head'), may hold values from 0 to 255
- junction_counts: int32 [8, 8, 8], P('interval', 'seq'), may hold values from 16 to 64, as said below
- pred_grad: float32 [8, 8, 8, 64], P('interval', 'seq', None, 'head'), may hold values from -6 to 6
Outputs:
- grad_input: bfloat16 [8, 2048, 1536], P('interval', 'seq', 'head')
- grad_query: bfloat16 [1536, 1536], P('head')
- grad_key: bfloat16 [1536, 1536], P('head')
- grad_value: bfloat16 [1536, 1536], P('head')
Inputs may be any that keep to these rules, and one draw needn't show every extreme that they name: `junction_counts`: slots at or past a bucket's count are empty. In each interval one acceptor shard, drawn from the seed, has 64 live slots from every donor shard; every other bucket has 16 to 32.
All inputs are finite; a program needn't handle non-finite values.
Results may differ from a plain program's by a relative error of at most 0.022.
Values may be sent and summed in bfloat16 or wider, within the bound.
No kernel may reach another device: no remote copies, remote signals or barrier semaphores. Data moves between devices by JAX's collectives and lax.ppermute only.
A program may use at most 64 MiB of HBM per device.

v0:
```python
import jax
import jax.numpy as jnp
from jax import lax
from jax.sharding import Mesh
from jax.sharding import PartitionSpec as P

HD = 192
PJ = 128
CORES = 2
F32 = jnp.float32
BF16 = jnp.bfloat16


def swap_cores(value):
    return lax.ppermute(value, "core", [(0, 1), (1, 0)])


def on_device(
    hidden_in,
    ctx_grad,
    w_query,
    w_key,
    w_value,
    w_junction,
    donor_pos,
    acceptor_pos,
    junction_counts,
    pred_grad,
):
    hidden = hidden_in[0]
    ctx = ctx_grad[0]
    tokens, width = hidden.shape
    chips = lax.axis_size("x")
    intervals = lax.axis_size("interval")
    core = lax.axis_index("core")
    half = chips * tokens
    softmax_scale = HD ** (-0.5)
    pair_scale = PJ ** (-0.5)

    def project(weight):
        return jnp.einsum("td,cd->tc", hidden, weight, preferred_element_type=F32).astype(BF16)

    queries, key_rows, value_rows = (project(w_query), project(w_key), project(w_value))
    features = jnp.dot(hidden, w_junction, preferred_element_type=F32).astype(BF16)
    sent = jnp.concatenate([key_rows, value_rows, features], axis=1)
    copies = jnp.broadcast_to(sent[None], (chips,) + sent.shape).reshape(half, -1)
    mine = lax.all_to_all(copies, "x", 0, 0, tiled=True)
    theirs = swap_cores(mine)
    both = jnp.concatenate([mine, theirs], axis=0)
    keys, values, all_features = (both[:, :HD], both[:, HD : 2 * HD], both[:, 2 * HD :])
    scores = jnp.einsum("qd,kd->qk", queries, keys, preferred_element_type=F32) * softmax_scale
    row_max = jnp.max(scores, axis=-1, keepdims=True)
    expd = jnp.exp(scores - row_max)
    probs = expd / jnp.sum(expd, axis=-1, keepdims=True)
    dprobs = jnp.einsum("qd,kd->qk", ctx, values, preferred_element_type=F32)
    row_delta = jnp.sum(probs * dprobs, axis=-1, keepdims=True)
    dscores_b = (probs * (dprobs - row_delta)).astype(BF16)
    probs_b = probs.astype(BF16)
    query_grad = (
        jnp.einsum("qk,kd->qd", dscores_b, keys, preferred_element_type=F32) * softmax_scale
    ).astype(BF16)
    key_term = (
        jnp.einsum("qk,qd->kd", dscores_b, queries, preferred_element_type=F32) * softmax_scale
    )
    value_term = jnp.einsum("qk,qd->kd", probs_b, ctx, preferred_element_type=F32)
    donor_idx = donor_pos[0, 0]
    buckets, slot_dev = donor_idx.shape
    slot_ids = lax.axis_index("head") * slot_dev + jnp.arange(slot_dev, dtype=jnp.int32)
    live_slots = slot_ids[None, :] < junction_counts[0, 0][:, None]
    shard = jnp.arange(buckets, dtype=jnp.int32)
    base = jnp.where(shard % CORES == core, 0, half) + shard // CORES * tokens
    accept_idx = base[:, None] + acceptor_pos[0, 0]
    donor_feat = features[donor_idx].astype(F32)
    accept_feat = all_features[accept_idx].astype(F32)
    pair_score = jnp.sum(donor_feat * accept_feat, axis=-1) * pair_scale
    slot_grad = (
        jnp.where(live_slots, pred_grad[0, 0] * jax.nn.sigmoid(pair_score), 0.0) * pair_scale
    )
    donor_term = slot_grad[..., None] * accept_feat
    accept_term = slot_grad[..., None] * donor_feat
    donor_sum = (
        jnp.zeros((tokens, PJ), F32).at[donor_idx.reshape(-1)].add(donor_term.reshape(-1, PJ))
    )
    spread = (
        jnp.zeros((CORES * half, PJ), F32)
        .at[accept_idx.reshape(-1)]
        .add(accept_term.reshape(-1, PJ))
    )
    terms = jnp.concatenate([key_term, value_term, spread], axis=1).astype(BF16)
    pair_sum = terms[:half].astype(F32) + swap_cores(terms[half:]).astype(F32)
    parts = lax.all_to_all(pair_sum.astype(BF16), "x", 0, 0, tiled=True)
    total = jnp.sum(parts.reshape(chips, tokens, -1).astype(F32), axis=0)
    key_grad = total[:, :HD].astype(BF16)
    value_grad = total[:, HD : 2 * HD].astype(BF16)
    feature_grad = (donor_sum + total[:, 2 * HD :]).astype(BF16)
    grads = jnp.concatenate([query_grad, key_grad, value_grad], axis=1)
    weights = jnp.concatenate([w_query, w_key, w_value], axis=0)
    input_term = jnp.dot(grads, weights, preferred_element_type=F32)
    input_term = input_term + jnp.einsum(
        "tp,dp->td", feature_grad, w_junction, preferred_element_type=F32
    )
    grad_input = lax.psum_scatter(input_term.astype(BF16), "head", scatter_dimension=1, tiled=True)
    rows = grads.shape[1]
    half_width = width // CORES
    weight_term = jnp.einsum("tc,td->cd", grads, hidden, preferred_element_type=F32).astype(BF16)

    def sum_parts(value, axis, count):
        got = lax.all_to_all(value, axis, 0, 0, tiled=True)
        return jnp.sum(got.reshape(count, -1, got.shape[-1]).astype(F32), axis=0).astype(BF16)

    term = weight_term.reshape(rows, CORES, half_width).transpose(1, 0, 2)
    term = sum_parts(term.reshape(CORES * rows, half_width), "core", CORES)
    term = sum_parts(term, "x", chips)
    part_rows = rows // chips
    cut = (2, part_rows // 2, intervals // 2, half_width // (intervals // 2))
    term = term.reshape(cut).transpose(0, 2, 1, 3).reshape(-1, cut[3])
    term = sum_parts(term, "interval", intervals)
    term = jnp.broadcast_to(term[None], (intervals,) + term.shape).reshape(-1, cut[3])
    term = lax.all_to_all(term, "interval", 0, 0, tiled=True)
    term = term.reshape(cut[0], cut[2], cut[1], cut[3]).transpose(0, 2, 1, 3)
    term = lax.all_gather(term.reshape(part_rows, half_width), "x", axis=0, tiled=True)
    other = swap_cores(term)
    left = jnp.where(core == 0, term, other)
    right = jnp.where(core == 0, other, term)
    whole = jnp.concatenate([left, right], axis=1)
    return (grad_input[None], whole[:HD], whole[HD : 2 * HD], whole[2 * HD :])


def solution(mesh):
    axes = (mesh.shape["interval"], mesh.shape["seq"] // CORES, CORES, mesh.shape["head"])
    split = Mesh(mesh.devices.reshape(axes), ("interval", "x", "core", "head"))
    seq = ("x", "core")
    placed = (
        P("interval", seq, None),
        P("interval", seq, "head"),
        P("head", None),
        P("head", None),
        P("head", None),
        P(),
        P("interval", seq, None, "head"),
        P("interval", seq, None, "head"),
        P("interval", seq, None),
        P("interval", seq, None, "head"),
    )
    return jax.shard_map(
        on_device,
        mesh=split,
        in_specs=placed,
        out_specs=(P("interval", seq, "head"), P("head", None), P("head", None), P("head", None)),
        check_vma=False,
    )
```

profile of v0, /device:TPU:2, one launch (start us, length us, event | category | flops | bytes accessed | tf_op | source)
XLA Modules:
  0.0 189.2 jit_solution(3122860435319958120)
XLA Ops:
  7.2 1.1 copy-done
  8.3 1.4 convolution_convert_fusion.5
  9.7 1.5 convolution_convert_fusion.2
  11.9 1.1 broadcast_in_dim.17
  12.9 9.4 %all-to-all-start = ((bf16[4,256,512]{2,1,0:T(8,128)(2,1)}), bf16[4,256,512]{2,1,0:T(8,128)(2,1)S(1)}, u32[]{:S(2)}, u32[]{:S(2)}) async-start(bf16[4,256,512]{2,1,0:T(8,128)(2,1)} %broadcast_in_dim.17), calls=%async_computation | async-start | bytes 2097152 | tf_op jit(solution)/shard_map/all_to_all | solution.py:47
  22.3 9.4 %all-to-all-done = bf16[4,256,512]{2,1,0:T(8,128)(2,1)S(1)} async-done(((bf16[4,256,512]{2,1,0:T(8,128)(2,1)}), bf16[4,256,512]{2,1,0:T(8,128)(2,1)S(1)}, u32[]{:S(2)}, u32[]{:S(2)}) %all-to-all-start) | async-done | bytes 1048608 | tf_op jit(solution)/shard_map/all_to_all | solution.py:47
  31.7 1.9 %collective-permute-start = (bf16[1024,512]{1,0:T(8,128)(2,1)S(1)}, bf16[1024,512]{1,0:T(8,128)(2,1)S(1)}, u32[]{:S(2)}, u32[]{:S(2)}) collective-permute-start(bf16[1024,512]{1,0:T(8,128)(2,1)S(1)} %bitcast.71), channel_id=1, source_target_pairs={{0,8},{8,0},{1,9},{9,1},{2,10},{10,2},{3,11},{11,3},{4,12},{12,4},... | collective-permute-start | bytes 3145736 | tf_op jit(solution)/shard_map/ppermute | solution.py:15
  33.8 0.9 copy.44
  36.6 0.7 lt.74
  37.3 0.7 lt.75
  38.6 0.7 add.139
  40.5 0.8 gather_fusion
  41.3 1.3 pad_clamp_fusion
  42.5 1.2 fusion.33
  45.6 1.5 convolution_convert_fusion.1
  47.1 1.0 multiply_reduce_fusion
  48.7 1.0 copy-done.1
  49.7 1.3 fusion.1
  51.1 0.6 gather_fusion.1
  51.9 2.0 %scatter_custom_fusion = f32[2048,128]{1,0:T(8,128)} fusion(s32[64]{0:T(128)} %fusion.33, f32[]{:T(128)} %constant.30.clone.1, bf16[64,128]{1,0:T(8,128)(2,1)S(1)} %gather_fusion, f32[64]{0:T(128)S(1)} %fusion.35), kind=kCustom, calls=%fused_computation.56 | custom fusion | flops 24576 | bytes 1065728 | tf_op jit(solution)/shard_map/scatter-add | solution.py:87
  53.9 1.4 copy.45
  55.3 1.5 pad_maximum_fusion
  57.0 2.4 %collective-permute-start.1 = (bf16[1024,512]{0,1:T(8,128)(2,1)S(1)}, bf16[1024,512]{0,1:T(8,128)(2,1)S(1)}, u32[]{:S(2)}, u32[]{:S(2)}) collective-permute-start(bf16[1024,512]{0,1:T(8,128)(2,1)S(1)} %slice.56), channel_id=1, source_target_pairs={{0,8},{8,0},{1,9},{9,1},{2,10},{10,2},{3,11},{11,3},{4,12},{12,4},... | collective-permute-start | bytes 3145736 | tf_op jit(solution)/shard_map/ppermute | solution.py:15
  59.4 2.3 %collective-permute-done.1 = bf16[1024,512]{0,1:T(8,128)(2,1)S(1)} collective-permute-done((bf16[1024,512]{0,1:T(8,128)(2,1)S(1)}, bf16[1024,512]{0,1:T(8,128)(2,1)S(1)}, u32[]{:S(2)}, u32[]{:S(2)}) %collective-permute-start.1) | collective-permute-done | bytes 1048608 | tf_op jit(solution)/shard_map/ppermute | solution.py:15
  62.1 1.1 copy.60
  63.1 5.7 %all-to-all-start.1 = ((bf16[4,256,512]{1,2,0:T(8,128)(2,1)}), bf16[4,256,512]{1,2,0:T(8,128)(2,1)}, u32[]{:S(2)}, u32[]{:S(2)}) async-start(bf16[4,256,512]{1,2,0:T(8,128)(2,1)} %bitcast.79), calls=%async_computation.1 | async-start | bytes 2097152 | tf_op jit(solution)/shard_map/all_to_all | solution.py:91
  68.8 1.8 fusion.10
  70.6 12.8 %all-to-all-done.1 = bf16[4,256,512]{1,2,0:T(8,128)(2,1)} async-done(((bf16[4,256,512]{1,2,0:T(8,128)(2,1)}), bf16[4,256,512]{1,2,0:T(8,128)(2,1)}, u32[]{:S(2)}, u32[]{:S(2)}) %all-to-all-start.1) | async-done | bytes 1048608 | tf_op jit(solution)/shard_map/all_to_all | solution.py:91
  83.3 1.4 convert_reduce_fusion
  84.8 0.8 copy-done.3
  85.6 0.6 convolution_convert_fusion
  86.4 5.2 %all_to_all.48 = bf16[2,576,768]{2,1,0:T(8,128)(2,1)S(1)} all-to-all(bf16[2,576,768]{2,1,0:T(8,128)(2,1)S(1)} %bitcast.76), channel_id=1, replica_groups=mesh['interval'=8,'x'=4,'core'=2,'head'=8] {'core'}, dimensions={0} | all-to-all | bytes 3538944 | tf_op jit(solution)/shard_map/all_to_all | solution.py:108
  91.5 0.9 reduce_sum.76
  92.4 16.5 %all_to_all.49 = bf16[4,144,768]{2,1,0:T(8,128)(2,1)S(1)} all-to-all(bf16[4,144,768]{2,1,0:T(8,128)(2,1)S(1)} %bitcast.80), channel_id=1, replica_groups=mesh['interval'=8,'x'=4,'core'=2,'head'=8] {'x'}, dimensions={0} | all-to-all | bytes 1769472 | tf_op jit(solution)/shard_map/all_to_all | solution.py:108
  109.3 0.7 copy.50
  110.1 6.7 %all-to-all-start.4 = ((bf16[8,72,192]{2,1,0:T(8,128)(2,1)}), bf16[8,72,192]{2,1,0:T(8,128)(2,1)S(1)}, u32[]{:S(2)}, u32[]{:S(2)}) async-start(bf16[8,72,192]{2,1,0:T(8,128)(2,1)} %bitcast.13), calls=%async_computation.5 | async-start | bytes 589824 | tf_op jit(solution)/shard_map/all_to_all | solution.py:108
  117.0 1.1 scatter_custom_fusion.1
  118.1 10.8 %all-to-all-done.4 = bf16[8,72,192]{2,1,0:T(8,128)(2,1)S(1)} async-done(((bf16[8,72,192]{2,1,0:T(8,128)(2,1)}), bf16[8,72,192]{2,1,0:T(8,128)(2,1)S(1)}, u32[]{:S(2)}, u32[]{:S(2)}) %all-to-all-start.4) | async-done | bytes 221216 | tf_op jit(solution)/shard_map/all_to_all | solution.py:108
  128.9 0.7 broadcast_in_dim.23
  129.7 3.4 %all-to-all-start.5 = ((bf16[8,72,192]{2,1,0:T(8,128)(2,1)}), bf16[8,72,192]{2,1,0:T(8,128)(2,1)S(1)}, u32[]{:S(2)}, u32[]{:S(2)}) async-start(bf16[8,72,192]{2,1,0:T(8,128)(2,1)} %broadcast_in_dim.23), calls=%async_computation.6 | async-start | bytes 589824 | tf_op jit(solution)/shard_map/all_to_all | solution.py:119
  133.2 2.0 %fusion.4 = f32[256,1536]{0,1:T(8,128)S(1)} fusion(bf16[192,1536]{1,0:T(8,128)(2,1)S(1)} %copy-done.6, bf16[192,1536]{1,0:T(8,128)(2,1)S(1)} %copy-done.8, bf16[192,1536]{1,0:T(8,128)(2,1)} %param.12, bf16[256,384]{0,1:T(8,128)(2,1)S(1)} %copy-done.5, bf16[256,192]{0,1:T(8,128)(2,1)S(1)} %fusion.10), kind=kOutput, calls=%fused_computation.29 | convolution fusion | flops 458883072 | bytes 3637248 | tf_op jit(solution)/shard_map/dot_general | solution.py:98
  135.3 1.2 fusion
  136.5 7.3 %all-to-all-done.5 = bf16[8,72,192]{2,1,0:T(8,128)(2,1)S(1)} async-done(((bf16[8,72,192]{2,1,0:T(8,128)(2,1)}), bf16[8,72,192]{2,1,0:T(8,128)(2,1)S(1)}, u32[]{:S(2)}, u32[]{:S(2)}) %all-to-all-start.5) | async-done | bytes 221216 | tf_op jit(solution)/shard_map/all_to_all | solution.py:119
  144.2 13.4 %all_gather.3 = bf16[576,768]{1,0:T(8,128)(2,1)S(1)} all-gather(bf16[144,768]{1,0:T(8,128)(2,1)S(1)} %reshape.268), channel_id=1, replica_groups=mesh['interval'=8,'x'=4,'core'=2,'head'=8] {'x'}, dimensions={0}, use_global_device_ids=true | all-gather | bytes 1105920 | tf_op jit(solution)/shard_map/all_gather | solution.py:121
  157.6 1.9 %collective-permute-start.2 = (bf16[576,768]{1,0:T(8,128)(2,1)S(1)}, bf16[576,768]{1,0:T(8,128)(2,1)S(1)}, u32[]{:S(2)}, u32[]{:S(2)}) collective-permute-start(bf16[576,768]{1,0:T(8,128)(2,1)S(1)} %all_gather.3), channel_id=1, source_target_pairs={{0,8},{8,0},{1,9},{9,1},{2,10},{10,2},{3,11},{11,3},{4,12},{12,4},... | collective-permute-start | bytes 2654216 | tf_op jit(solution)/shard_map/ppermute | solution.py:15
  159.6 2.4 %collective-permute-done.2 = bf16[576,768]{1,0:T(8,128)(2,1)S(1)} collective-permute-done((bf16[576,768]{1,0:T(8,128)(2,1)S(1)}, bf16[576,768]{1,0:T(8,128)(2,1)S(1)}, u32[]{:S(2)}, u32[]{:S(2)}) %collective-permute-start.2) | collective-permute-done | bytes 884768 | tf_op jit(solution)/shard_map/ppermute | solution.py:15
  162.1 1.2 pad_maximum_fusion.1
  163.3 19.0 %reduce-scatter.2.cloned.1.call-done = bf16[256,192]{0,1:T(8,128)(2,1)} async-done(((bf16[256,1536]{0,1:T(8,128)(2,1)}), bf16[256,192]{0,1:T(8,128)(2,1)}) %reduce-scatter.2.cloned.1.call-update) | async-done | bytes 98320 | tf_op jit(solution)/shard_map/reduce_scatter | solution.py:102
  (83 shorter events, 8.9 us)
Async XLA Ops:
  7.2 1.1 copy-start
  7.2 4.0 %copy-start.7 = (bf16[192,1536]{1,0:T(8,128)(2,1)S(1)}, bf16[192,1536]{1,0:T(8,128)(2,1)}, u32[]{:S(2)}) copy-start(bf16[192,1536]{1,0:T(8,128)(2,1)} %param.13) | copy-start | bytes 1769476
  9.7 1.9 %copy-start.10 = (bf16[256,128]{0,1:T(8,128)(2,1)}, bf16[256,128]{0,1:T(8,128)(2,1)S(1)}, u32[]{:S(2)}) copy-start(bf16[256,128]{0,1:T(8,128)(2,1)S(1)} %convolution_convert_fusion.5) | copy-start | bytes 196612
  11.7 22.0 %copy-start.12 = (s32[1,1,8,8]{3,2,1,0:T(8,128)S(1)}, s32[1,1,8,8]{3,2,1,0:T(8,128)}, u32[]{:S(2)}) copy-start(s32[1,1,8,8]{3,2,1,0:T(8,128)} %param.17) | copy-start | bytes 772
  11.7 24.2 %copy-start.13 = (s32[1,1,8,8]{3,2,1,0:T(8,128)S(1)}, s32[1,1,8,8]{3,2,1,0:T(8,128)}, u32[]{:S(2)}) copy-start(s32[1,1,8,8]{3,2,1,0:T(8,128)} %param.16) | copy-start | bytes 772
  11.7 26.3 %copy-start.17 = (f32[1,1,8,8]{3,2,1,0:T(8,128)S(1)}, f32[1,1,8,8]{3,2,1,0:T(8,128)}, u32[]{:S(2)}) copy-start(f32[1,1,8,8]{3,2,1,0:T(8,128)} %param.19) | copy-start | bytes 772
  11.7 32.0 %copy-start.9 = (bf16[192,1536]{1,0:T(8,128)(2,1)S(1)}, bf16[192,1536]{1,0:T(8,128)(2,1)}, u32[]{:S(2)}) copy-start(bf16[192,1536]{1,0:T(8,128)(2,1)} %param.12) | copy-start | bytes 1769476
  12.9 18.8 %all-to-all-start = ((bf16[4,256,512]{2,1,0:T(8,128)(2,1)}), bf16[4,256,512]{2,1,0:T(8,128)(2,1)S(1)}, u32[]{:S(2)}, u32[]{:S(2)}) async-start(bf16[4,256,512]{2,1,0:T(8,128)(2,1)} %broadcast_in_dim.17), calls=%async_computation | async-start | bytes 2097152 | tf_op jit(solution)/shard_map/all_to_all | solution.py:47
  22.3 11.4 %copy-start.21 = (s32[8]{0:T(128)}, s32[8]{0:T(128)S(1)}, u32[]{:S(2)}) copy-start(s32[8]{0:T(128)S(1)} %fusion.31) | copy-start | bytes 100
  31.7 12.4 %collective-permute-start = (bf16[1024,512]{1,0:T(8,128)(2,1)S(1)}, bf16[1024,512]{1,0:T(8,128)(2,1)S(1)}, u32[]{:S(2)}, u32[]{:S(2)}) collective-permute-start(bf16[1024,512]{1,0:T(8,128)(2,1)S(1)} %bitcast.71), channel_id=1, source_target_pairs={{0,8},{8,0},{1,9},{9,1},{2,10},{10,2},{3,11},{11,3},{4,12},{12,4},... | collective-permute-start | bytes 3145736 | tf_op jit(solution)/shard_map/ppermute | solution.py:15
  44.7 0.9 copy-start.22
  48.7 1.0 copy-start.1
  49.7 1.4 copy-start.11
  49.7 2.1 %copy-start.18 = (s32[64]{0:T(128)S(1)}, s32[64]{0:T(128)}, u32[]{:S(2)}) copy-start(s32[64]{0:T(128)} %lt.72) | copy-start | bytes 772
  49.7 2.1 %copy-start.19 = (s32[64]{0:T(128)S(1)}, s32[64]{0:T(128)}, u32[]{:S(2)}) copy-start(s32[64]{0:T(128)} %lt.75) | copy-start | bytes 772
  49.7 2.1 %copy-start.20 = (f32[64]{0:T(128)S(1)}, f32[64]{0:T(128)}, u32[]{:S(2)}) copy-start(f32[64]{0:T(128)} %squeeze.20) | copy-start | bytes 772
  51.9 5.0 %copy-start.15 = (f32[64]{0:T(128)}, f32[64]{0:T(128)S(1)}, u32[]{:S(2)}) copy-start(f32[64]{0:T(128)S(1)} %fusion.35) | copy-start | bytes 772
  57.0 4.7 %collective-permute-start.1 = (bf16[1024,512]{0,1:T(8,128)(2,1)S(1)}, bf16[1024,512]{0,1:T(8,128)(2,1)S(1)}, u32[]{:S(2)}, u32[]{:S(2)}) collective-permute-start(bf16[1024,512]{0,1:T(8,128)(2,1)S(1)} %slice.56), channel_id=1, source_target_pairs={{0,8},{8,0},{1,9},{9,1},{2,10},{10,2},{3,11},{11,3},{4,12},{12,4},... | collective-permute-start | bytes 3145736 | tf_op jit(solution)/shard_map/ppermute | solution.py:15
  63.1 20.2 %all-to-all-start.1 = ((bf16[4,256,512]{1,2,0:T(8,128)(2,1)}), bf16[4,256,512]{1,2,0:T(8,128)(2,1)}, u32[]{:S(2)}, u32[]{:S(2)}) async-start(bf16[4,256,512]{1,2,0:T(8,128)(2,1)} %bitcast.79), calls=%async_computation.1 | async-start | bytes 2097152 | tf_op jit(solution)/shard_map/all_to_all | solution.py:91
  84.8 0.8 copy-start.3
  85.6 0.7 copy-start.4
  92.4 24.4 %copy-start.14 = (s32[1,1,8,8]{3,2,1,0:T(8,128)S(1)}, s32[1,1,8,8]{3,2,1,0:T(8,128)}, u32[]{:S(2)}) copy-start(s32[1,1,8,8]{3,2,1,0:T(8,128)} %param.16) | copy-start | bytes 772
  92.4 24.5 %slice-start = ((f32[256,512]{0,1:T(8,128)}), f32[256,128]{0,1:T(8,128)S(1)}, s32[]{:S(2)}) async-start(f32[256,512]{0,1:T(8,128)} %copy-done.3), calls=%async_computation.8 | async-start | bytes 262144 | tf_op jit(solution)/shard_map/slice | solution.py:95
  108.9 8.1 %copy-start.16 = (f32[64]{0:T(128)S(1)}, f32[64]{0:T(128)}, u32[]{:S(2)}) copy-start(f32[64]{0:T(128)} %copy-done.15) | copy-start | bytes 772
  108.9 24.3 %copy-start.5 = (bf16[256,384]{0,1:T(8,128)(2,1)S(1)}, bf16[256,384]{0,1:T(8,128)(2,1)}, u32[]{:S(2)}) copy-start(bf16[256,384]{0,1:T(8,128)(2,1)} %copy-done.4) | copy-start | bytes 589828
  108.9 24.3 %copy-start.6 = (bf16[192,1536]{1,0:T(8,128)(2,1)S(1)}, bf16[192,1536]{1,0:T(8,128)(2,1)}, u32[]{:S(2)}) copy-start(bf16[192,1536]{1,0:T(8,128)(2,1)} %param.14) | copy-start | bytes 1769476
  109.1 24.1 %copy-start.8 = (bf16[192,1536]{1,0:T(8,128)(2,1)S(1)}, bf16[192,1536]{1,0:T(8,128)(2,1)}, u32[]{:S(2)}) copy-start(bf16[192,1536]{1,0:T(8,128)(2,1)} %param.13) | copy-start | bytes 1769476
  110.1 18.8 %all-to-all-start.4 = ((bf16[8,72,192]{2,1,0:T(8,128)(2,1)}), bf16[8,72,192]{2,1,0:T(8,128)(2,1)S(1)}, u32[]{:S(2)}, u32[]{:S(2)}) async-start(bf16[8,72,192]{2,1,0:T(8,128)(2,1)} %bitcast.13), calls=%async_computation.5 | async-start | bytes 589824 | tf_op jit(solution)/shard_map/all_to_all | solution.py:108
  129.7 14.2 %all-to-all-start.5 = ((bf16[8,72,192]{2,1,0:T(8,128)(2,1)}), bf16[8,72,192]{2,1,0:T(8,128)(2,1)S(1)}, u32[]{:S(2)}, u32[]{:S(2)}) async-start(bf16[8,72,192]{2,1,0:T(8,128)(2,1)} %broadcast_in_dim.23), calls=%async_computation.6 | async-start | bytes 589824 | tf_op jit(solution)/shard_map/all_to_all | solution.py:119
  133.1 2.1 %copy-start.2 = (bf16[1536,128]{1,0:T(8,128)(2,1)S(1)}, bf16[1536,128]{1,0:T(8,128)(2,1)}, u32[]{:S(2)}) copy-start(bf16[1536,128]{1,0:T(8,128)(2,1)} %param.15) | copy-start | bytes 1179652
  133.1 49.2 %reduce-scatter.2.cloned.1.call-start = ((), (), s32[]{:S(2)}) async-start(), calls=%async_computation.7 | async-start | bytes 884736 | tf_op jit(solution)/shard_map/reduce_scatter | solution.py:102
  157.6 4.3 %collective-permute-start.2 = (bf16[576,768]{1,0:T(8,128)(2,1)S(1)}, bf16[576,768]{1,0:T(8,128)(2,1)S(1)}, u32[]{:S(2)}, u32[]{:S(2)}) collective-permute-start(bf16[576,768]{1,0:T(8,128)(2,1)S(1)} %all_gather.3), channel_id=1, source_target_pairs={{0,8},{8,0},{1,9},{9,1},{2,10},{10,2},{3,11},{11,3},{4,12},{12,4},... | collective-permute-start | bytes 2654216 | tf_op jit(solution)/shard_map/ppermute | solution.py:15
Sparse Core Ops, SparseCore 0:
  137.4 44.9 reduce-scatter.1
where the time goes:
time: 190 us; the launch traced here: 189 us
  waiting for transfers between devices  64 us (34%)
  blocking collectives  35 us (18%)
  starting transfers between devices  31.5 us (17%)
  local copies, waits for them, and re-layouts  17.2 us (9%)
  between operations  14.5 us (8%)
  matrix products  13.7 us (7%)
  other arithmetic  13.2 us (7%)
    all_to_all x2, blocking collectives, sum_parts(): got = lax.all_to_all(value, axis, 0, 0, tiled=True)  21.6 us
    reduce_scatter x1, waiting for transfers between devices, on_device(): lax.psum_scatter(input_term.astype(BF16), 'head', scatter_dimension=1, ti...  19 us
    all_gather x1, blocking collectives, on_device(): lax.all_gather(term.reshape(part_rows, half_width), 'x', axis=0, tiled=True)  13.4 us
    all_to_all x1, waiting for transfers between devices, on_device(): parts = lax.all_to_all(pair_sum.astype(BF16), 'x', 0, 0, tiled=True)  12.8 us
    all_to_all x1, waiting for transfers between devices, sum_parts(): got = lax.all_to_all(value, axis, 0, 0, tiled=True)  10.8 us
    all_to_all x1, waiting for transfers between devices, on_device(): mine = lax.all_to_all(copies, 'x', 0, 0, tiled=True)  9.43 us
    all_to_all x1, starting transfers between devices, on_device(): mine = lax.all_to_all(copies, 'x', 0, 0, tiled=True)  9.39 us
    all_to_all x1, waiting for transfers between devices, on_device(): term = lax.all_to_all(term, 'interval', 0, 0, tiled=True)  7.32 us
  transfers between devices with their start and end apart: 8, of which 7 were waited for; matrix products, arithmetic and copies ran while one was open for 10% of the time, Pallas kernels for 0%

commit v1 on v0

--- a/solution.py
+++ b/solution.py
@@ -118,7 +118,12 @@
     term = jnp.broadcast_to(term[None], (intervals,) + term.shape).reshape(-1, cut[3])
     term = lax.all_to_all(term, "interval", 0, 0, tiled=True)
     term = term.reshape(cut[0], cut[2], cut[1], cut[3]).transpose(0, 2, 1, 3)
-    term = lax.all_gather(term.reshape(part_rows, half_width), "x", axis=0, tiled=True)
+    term = jnp.concatenate(
+        lax.all_to_all(
+            jnp.stack([term.reshape(part_rows, half_width)] * lax.axis_size("x")), "x", 0, 0
+        ),
+        axis=0,
+    )
     other = swap_cores(term)
     left = jnp.where(core == 0, term, other)
     right = jnp.where(core == 0, other, term)

time: 190 us -> 202 us (1.063)
  waiting for transfers between devices: 64 us -> 72.6 us
  blocking collectives: 35 us -> 40.1 us
    all_to_all x2 -> x3, blocking collectives: 21.6 us -> 40.1 us  [sum_parts(): got = lax.all_to_all(value, axis, 0, 0, tiled=True)]
    all_gather x1 -> x0, blocking collectives: 13.4 us -> none  [on_device(): lax.all_gather(term.reshape(part_rows, half_width), 'x', axis=0, tiled=True)]
    reduce_scatter x1, waiting for transfers between devices: 19 us -> 31.1 us  [on_device(): lax.psum_scatter(input_term.astype(BF16), 'head', scatter_dimension=1, ti...]
    all_to_all x1, waiting for transfers between devices: 10.8 us -> 4 us  [on_device(): lax.all_to_all(jnp.stack([term.reshape(part_rows, half_width)] * lax.axis...]
    all_to_all x1, waiting for transfers between devices: 7.32 us -> 10.7 us  [on_device(): term = lax.all_to_all(term, 'interval', 0, 0, tiled=True)]
  transfers between devices with their start and end apart: 8 -> 8, of which waited for: 7 -> 7; matrix products, arithmetic and copies ran while one was open for 10% -> 9% of each run, Pallas kernels for 0% -> 0%
where the time goes in v1:
time: 202 us; the launch traced here: 201 us
  waiting for transfers between devices  72.6 us (36%)
  blocking collectives  40.1 us (20%)
  starting transfers between devices  29.6 us (15%)
  local copies, waits for them, and re-layouts  17.5 us (9%)
  between operations  14.5 us (7%)
  matrix products  13.8 us (7%)
  other arithmetic  13.3 us (7%)
    all_to_all x3, blocking collectives, sum_parts(): got = lax.all_to_all(value, axis, 0, 0, tiled=True)  40.1 us
    reduce_scatter x1, waiting for transfers between devices, on_device(): lax.psum_scatter(input_term.astype(BF16), 'head', scatter_dimension=1, ti...  31.1 us
    all_to_all x1, waiting for transfers between devices, on_device(): parts = lax.all_to_all(pair_sum.astype(BF16), 'x', 0, 0, tiled=True)  12.8 us
    all_to_all x1, waiting for transfers between devices, on_device(): term = lax.all_to_all(term, 'interval', 0, 0, tiled=True)  10.7 us
    all_to_all x1, waiting for transfers between devices, on_device(): mine = lax.all_to_all(copies, 'x', 0, 0, tiled=True)  9.43 us
    all_to_all x1, starting transfers between devices, on_device(): mine = lax.all_to_all(copies, 'x', 0, 0, tiled=True)  9.39 us
    ppermute x3, starting transfers between devices, swap_cores(): return lax.ppermute(value, 'core', [(0, 1), (1, 0)])  6.22 us
    all_to_all x1, starting transfers between devices, on_device(): parts = lax.all_to_all(pair_sum.astype(BF16), 'x', 0, 0, tiled=True)  5.68 us
  transfers between devices with their start and end apart: 8, of which 7 were waited for; matrix products, arithmetic and copies ran while one was open for 9% of the time, Pallas kernels for 0%

profile of v1, /device:TPU:2, one launch (start us, length us, event | category | flops | bytes accessed | tf_op | source)
XLA Modules:
  0.0 201.4 jit_solution(5144197465520426676)
XLA Ops:
  7.2 1.1 copy-done
  8.3 1.4 convolution_convert_fusion.5
  9.7 1.5 convolution_convert_fusion.2
  11.9 1.1 broadcast_in_dim.17
  12.9 9.4 %all-to-all-start = ((bf16[4,256,512]{2,1,0:T(8,128)(2,1)}), bf16[4,256,512]{2,1,0:T(8,128)(2,1)S(1)}, u32[]{:S(2)}, u32[]{:S(2)}) async-start(bf16[4,256,512]{2,1,0:T(8,128)(2,1)} %broadcast_in_dim.17), calls=%async_computation | async-start | bytes 2097152 | tf_op jit(solution)/shard_map/all_to_all | solution.py:47
  22.3 9.4 %all-to-all-done = bf16[4,256,512]{2,1,0:T(8,128)(2,1)S(1)} async-done(((bf16[4,256,512]{2,1,0:T(8,128)(2,1)}), bf16[4,256,512]{2,1,0:T(8,128)(2,1)S(1)}, u32[]{:S(2)}, u32[]{:S(2)}) %all-to-all-start) | async-done | bytes 1048608 | tf_op jit(solution)/shard_map/all_to_all | solution.py:47
  31.7 1.9 collective-permute-start
  33.8 0.9 copy.44
  36.6 0.7 lt.74
  37.3 0.7 lt.75
  38.6 0.7 add.139
  40.5 0.8 gather_fusion
  41.3 1.3 pad_clamp_fusion
  42.5 1.2 fusion.33
  45.6 1.5 convolution_convert_fusion.1
  47.1 1.0 multiply_reduce_fusion
  48.7 1.0 copy-done.1
  49.7 1.3 fusion.1
  51.1 0.6 gather_fusion.1
  51.9 2.0 %scatter_custom_fusion = f32[2048,128]{1,0:T(8,128)} fusion(s32[64]{0:T(128)} %fusion.33, f32[]{:T(128)} %constant.30.clone.1, bf16[64,128]{1,0:T(8,128)(2,1)S(1)} %gather_fusion, f32[64]{0:T(128)S(1)} %fusion.35), kind=kCustom, calls=%fused_computation.56 | custom fusion | flops 24576 | bytes 1065728 | tf_op jit(solution)/shard_map/scatter-add | solution.py:87
  53.9 1.4 copy.45
  55.3 1.5 pad_maximum_fusion
  57.0 2.4 %collective-permute-start.1 = (bf16[1024,512]{0,1:T(8,128)(2,1)S(1)}, bf16[1024,512]{0,1:T(8,128)(2,1)S(1)}, u32[]{:S(2)}, u32[]{:S(2)}) collective-permute-start(bf16[1024,512]{0,1:T(8,128)(2,1)S(1)} %slice.56), channel_id=1, source_target_pairs={{0,8},{8,0},{1,9},{9,1},{2,10},{10,2},{3,11},{11,3},{4,12},{12,4},... | collective-permute-start | bytes 3145736 | tf_op jit(solution)/shard_map/ppermute | solution.py:15
  59.4 2.3 %collective-permute-done.1 = bf16[1024,512]{0,1:T(8,128)(2,1)S(1)} collective-permute-done((bf16[1024,512]{0,1:T(8,128)(2,1)S(1)}, bf16[1024,512]{0,1:T(8,128)(2,1)S(1)}, u32[]{:S(2)}, u32[]{:S(2)}) %collective-permute-start.1) | collective-permute-done | bytes 1048608 | tf_op jit(solution)/shard_map/ppermute | solution.py:15
  62.1 1.1 copy.60
  63.1 5.7 %all-to-all-start.1 = ((bf16[4,256,512]{1,2,0:T(8,128)(2,1)}), bf16[4,256,512]{1,2,0:T(8,128)(2,1)}, u32[]{:S(2)}, u32[]{:S(2)}) async-start(bf16[4,256,512]{1,2,0:T(8,128)(2,1)} %bitcast.82), calls=%async_computation.1 | async-start | bytes 2097152 | tf_op jit(solution)/shard_map/all_to_all | solution.py:91
  68.8 1.8 fusion.10
  70.6 12.8 %all-to-all-done.1 = bf16[4,256,512]{1,2,0:T(8,128)(2,1)} async-done(((bf16[4,256,512]{1,2,0:T(8,128)(2,1)}), bf16[4,256,512]{1,2,0:T(8,128)(2,1)}, u32[]{:S(2)}, u32[]{:S(2)}) %all-to-all-start.1) | async-done | bytes 1048608 | tf_op jit(solution)/shard_map/all_to_all | solution.py:91
  83.3 1.4 convert_reduce_fusion
  84.8 0.8 copy-done.3
  85.6 0.6 convolution_convert_fusion
  86.4 5.2 %all_to_all.53 = bf16[2,576,768]{2,1,0:T(8,128)(2,1)S(1)} all-to-all(bf16[2,576,768]{2,1,0:T(8,128)(2,1)S(1)} %bitcast.79), channel_id=1, replica_groups=mesh['interval'=8,'x'=4,'core'=2,'head'=8] {'core'}, dimensions={0} | all-to-all | bytes 3538944 | tf_op jit(solution)/shard_map/all_to_all | solution.py:108
  91.5 0.9 reduce_sum.76
  92.4 16.3 %all_to_all.54 = bf16[4,144,768]{2,1,0:T(8,128)(2,1)S(1)} all-to-all(bf16[4,144,768]{2,1,0:T(8,128)(2,1)S(1)} %bitcast.83), channel_id=1, replica_groups=mesh['interval'=8,'x'=4,'core'=2,'head'=8] {'x'}, dimensions={0} | all-to-all | bytes 1769472 | tf_op jit(solution)/shard_map/all_to_all | solution.py:108
  109.2 18.6 %all_to_all.55 = bf16[8,72,192]{2,1,0:T(8,128)(2,1)S(1)} all-to-all(bf16[8,72,192]{2,1,0:T(8,128)(2,1)S(1)} %bitcast.86), channel_id=1, replica_groups=mesh['interval'=8,'x'=4,'core'=2,'head'=8] {'interval'}, dimensions={0} | all-to-all | bytes 442368 | tf_op jit(solution)/shard_map/all_to_all | solution.py:108
  127.9 0.7 broadcast_in_dim.23
  128.6 3.4 %all-to-all-start.5 = ((bf16[8,72,192]{2,1,0:T(8,128)(2,1)}), bf16[8,72,192]{2,1,0:T(8,128)(2,1)S(1)}, u32[]{:S(2)}, u32[]{:S(2)}) async-start(bf16[8,72,192]{2,1,0:T(8,128)(2,1)} %broadcast_in_dim.23), calls=%async_computation.6 | async-start | bytes 589824 | tf_op jit(solution)/shard_map/all_to_all | solution.py:119
  132.1 10.7 %all-to-all-done.5 = bf16[8,72,192]{2,1,0:T(8,128)(2,1)S(1)} async-done(((bf16[8,72,192]{2,1,0:T(8,128)(2,1)}), bf16[8,72,192]{2,1,0:T(8,128)(2,1)S(1)}, u32[]{:S(2)}, u32[]{:S(2)}) %all-to-all-start.5) | async-done | bytes 221216 | tf_op jit(solution)/shard_map/all_to_all | solution.py:119
  143.2 1.0 stack.3
  144.2 4.9 %all-to-all-start.6 = ((bf16[4,144,768]{2,1,0:T(8,128)(2,1)}), bf16[4,144,768]{2,1,0:T(8,128)(2,1)S(1)}, u32[]{:S(2)}, u32[]{:S(2)}) async-start(bf16[4,144,768]{2,1,0:T(8,128)(2,1)} %stack.3), calls=%async_computation.7 | async-start | bytes 1769472 | tf_op jit(solution)/shard_map/all_to_all | solution.py:122
  149.2 1.1 scatter_custom_fusion.1
  150.4 2.1 %fusion.4 = f32[256,1536]{0,1:T(8,128)S(1)} fusion(bf16[192,1536]{1,0:T(8,128)(2,1)S(1)} %copy-done.6, bf16[192,1536]{1,0:T(8,128)(2,1)S(1)} %copy-done.8, bf16[192,1536]{1,0:T(8,128)(2,1)} %param.12, bf16[256,384]{0,1:T(8,128)(2,1)S(1)} %copy-done.5, bf16[256,192]{0,1:T(8,128)(2,1)S(1)} %fusion.10), kind=kOutput, calls=%fused_computation.29 | convolution fusion | flops 458883072 | bytes 3637248 | tf_op jit(solution)/shard_map/dot_general | solution.py:98
  152.4 1.3 fusion
  153.8 4.0 %all-to-all-done.6 = bf16[4,144,768]{2,1,0:T(8,128)(2,1)S(1)} async-done(((bf16[4,144,768]{2,1,0:T(8,128)(2,1)}), bf16[4,144,768]{2,1,0:T(8,128)(2,1)S(1)}, u32[]{:S(2)}, u32[]{:S(2)}) %all-to-all-start.6) | async-done | bytes 884768 | tf_op jit(solution)/shard_map/all_to_all | solution.py:122
  157.8 1.9 collective-permute-start.2
  159.7 2.4 %collective-permute-done.2 = bf16[576,768]{1,0:T(8,128)(2,1)S(1)} collective-permute-done((bf16[576,768]{1,0:T(8,128)(2,1)S(1)}, bf16[576,768]{1,0:T(8,128)(2,1)S(1)}, u32[]{:S(2)}, u32[]{:S(2)}) %collective-permute-start.2) | collective-permute-done | bytes 884768 | tf_op jit(solution)/shard_map/ppermute | solution.py:15
  162.2 1.2 pad_maximum_fusion.1
  163.5 31.1 %reduce-scatter.2.cloned.1.call-done = bf16[256,192]{0,1:T(8,128)(2,1)} async-done(((bf16[256,1536]{0,1:T(8,128)(2,1)}), bf16[256,192]{0,1:T(8,128)(2,1)}) %reduce-scatter.2.cloned.1.call-update) | async-done | bytes 98320 | tf_op jit(solution)/shard_map/reduce_scatter | solution.py:102
  (84 shorter events, 9.0 us)
Async XLA Ops:
  7.2 1.1 copy-start
  7.2 4.0 %copy-start.7 = (bf16[192,1536]{1,0:T(8,128)(2,1)S(1)}, bf16[192,1536]{1,0:T(8,128)(2,1)}, u32[]{:S(2)}) copy-start(bf16[192,1536]{1,0:T(8,128)(2,1)} %param.13) | copy-start | bytes 1769476
  9.7 1.9 copy-start.10
  11.7 22.0 %copy-start.12 = (s32[1,1,8,8]{3,2,1,0:T(8,128)S(1)}, s32[1,1,8,8]{3,2,1,0:T(8,128)}, u32[]{:S(2)}) copy-start(s32[1,1,8,8]{3,2,1,0:T(8,128)} %param.17) | copy-start | bytes 772
  11.7 24.2 %copy-start.13 = (s32[1,1,8,8]{3,2,1,0:T(8,128)S(1)}, s32[1,1,8,8]{3,2,1,0:T(8,128)}, u32[]{:S(2)}) copy-start(s32[1,1,8,8]{3,2,1,0:T(8,128)} %param.16) | copy-start | bytes 772
  11.7 26.3 %copy-start.17 = (f32[1,1,8,8]{3,2,1,0:T(8,128)S(1)}, f32[1,1,8,8]{3,2,1,0:T(8,128)}, u32[]{:S(2)}) copy-start(f32[1,1,8,8]{3,2,1,0:T(8,128)} %param.19) | copy-start | bytes 772
  11.7 32.0 %copy-start.9 = (bf16[192,1536]{1,0:T(8,128)(2,1)S(1)}, bf16[192,1536]{1,0:T(8,128)(2,1)}, u32[]{:S(2)}) copy-start(bf16[192,1536]{1,0:T(8,128)(2,1)} %param.12) | copy-start | bytes 1769476
  12.9 18.8 %all-to-all-start = ((bf16[4,256,512]{2,1,0:T(8,128)(2,1)}), bf16[4,256,512]{2,1,0:T(8,128)(2,1)S(1)}, u32[]{:S(2)}, u32[]{:S(2)}) async-start(bf16[4,256,512]{2,1,0:T(8,128)(2,1)} %broadcast_in_dim.17), calls=%async_computation | async-start | bytes 2097152 | tf_op jit(solution)/shard_map/all_to_all | solution.py:47
  22.3 11.4 %copy-start.21 = (s32[8]{0:T(128)}, s32[8]{0:T(128)S(1)}, u32[]{:S(2)}) copy-start(s32[8]{0:T(128)S(1)} %fusion.31) | copy-start | bytes 100
  31.7 12.4 %collective-permute-start = (bf16[1024,512]{1,0:T(8,128)(2,1)S(1)}, bf16[1024,512]{1,0:T(8,128)(2,1)S(1)}, u32[]{:S(2)}, u32[]{:S(2)}) collective-permute-start(bf16[1024,512]{1,0:T(8,128)(2,1)S(1)} %bitcast.74), channel_id=1, source_target_pairs={{0,8},{8,0},{1,9},{9,1},{2,10},{10,2},{3,11},{11,3},{4,12},{12,4},... | collective-permute-start | bytes 3145736 | tf_op jit(solution)/shard_map/ppermute | solution.py:15
  44.7 0.9 copy-start.22
  48.7 1.0 copy-start.1
  49.7 1.4 copy-start.11
  49.7 2.1 %copy-start.18 = (s32[64]{0:T(128)S(1)}, s32[64]{0:T(128)}, u32[]{:S(2)}) copy-start(s32[64]{0:T(128)} %lt.72) | copy-start | bytes 772
  49.7 2.1 %copy-start.19 = (s32[64]{0:T(128)S(1)}, s32[64]{0:T(128)}, u32[]{:S(2)}) copy-start(s32[64]{0:T(128)} %lt.75) | copy-start | bytes 772
  49.7 2.1 %copy-start.20 = (f32[64]{0:T(128)S(1)}, f32[64]{0:T(128)}, u32[]{:S(2)}) copy-start(f32[64]{0:T(128)} %squeeze.20) | copy-start | bytes 772
  51.9 5.0 %copy-start.15 = (f32[64]{0:T(128)}, f32[64]{0:T(128)S(1)}, u32[]{:S(2)}) copy-start(f32[64]{0:T(128)S(1)} %fusion.35) | copy-start | bytes 772
  57.0 4.7 %collective-permute-start.1 = (bf16[1024,512]{0,1:T(8,128)(2,1)S(1)}, bf16[1024,512]{0,1:T(8,128)(2,1)S(1)}, u32[]{:S(2)}, u32[]{:S(2)}) collective-permute-start(bf16[1024,512]{0,1:T(8,128)(2,1)S(1)} %slice.56), channel_id=1, source_target_pairs={{0,8},{8,0},{1,9},{9,1},{2,10},{10,2},{3,11},{11,3},{4,12},{12,4},... | collective-permute-start | bytes 3145736 | tf_op jit(solution)/shard_map/ppermute | solution.py:15
  63.1 20.2 %all-to-all-start.1 = ((bf16[4,256,512]{1,2,0:T(8,128)(2,1)}), bf16[4,256,512]{1,2,0:T(8,128)(2,1)}, u32[]{:S(2)}, u32[]{:S(2)}) async-start(bf16[4,256,512]{1,2,0:T(8,128)(2,1)} %bitcast.82), calls=%async_computation.1 | async-start | bytes 2097152 | tf_op jit(solution)/shard_map/all_to_all | solution.py:91
  84.8 0.8 copy-start.3
  85.6 0.7 copy-start.4
  108.8 23.3 %copy-start.14 = (s32[1,1,8,8]{3,2,1,0:T(8,128)S(1)}, s32[1,1,8,8]{3,2,1,0:T(8,128)}, u32[]{:S(2)}) copy-start(s32[1,1,8,8]{3,2,1,0:T(8,128)} %param.16) | copy-start | bytes 772
  128.6 14.2 %all-to-all-start.5 = ((bf16[8,72,192]{2,1,0:T(8,128)(2,1)}), bf16[8,72,192]{2,1,0:T(8,128)(2,1)S(1)}, u32[]{:S(2)}, u32[]{:S(2)}) async-start(bf16[8,72,192]{2,1,0:T(8,128)(2,1)} %broadcast_in_dim.23), calls=%async_computation.6 | async-start | bytes 589824 | tf_op jit(solution)/shard_map/all_to_all | solution.py:119
  142.8 6.4 %slice-start = ((f32[256,512]{0,1:T(8,128)}), f32[256,128]{0,1:T(8,128)S(1)}, s32[]{:S(2)}) async-start(f32[256,512]{0,1:T(8,128)} %copy-done.3), calls=%async_computation.9 | async-start | bytes 262144 | tf_op jit(solution)/shard_map/slice | solution.py:95
  142.9 6.3 %copy-start.16 = (f32[64]{0:T(128)S(1)}, f32[64]{0:T(128)}, u32[]{:S(2)}) copy-start(f32[64]{0:T(128)} %copy-done.15) | copy-start | bytes 772
  142.9 7.4 %copy-start.5 = (bf16[256,384]{0,1:T(8,128)(2,1)S(1)}, bf16[256,384]{0,1:T(8,128)(2,1)}, u32[]{:S(2)}) copy-start(bf16[256,384]{0,1:T(8,128)(2,1)} %copy-done.4) | copy-start | bytes 589828
  142.9 7.4 %copy-start.6 = (bf16[192,1536]{1,0:T(8,128)(2,1)S(1)}, bf16[192,1536]{1,0:T(8,128)(2,1)}, u32[]{:S(2)}) copy-start(bf16[192,1536]{1,0:T(8,128)(2,1)} %param.14) | copy-start | bytes 1769476
  142.9 7.4 %copy-start.8 = (bf16[192,1536]{1,0:T(8,128)(2,1)S(1)}, bf16[192,1536]{1,0:T(8,128)(2,1)}, u32[]{:S(2)}) copy-start(bf16[192,1536]{1,0:T(8,128)(2,1)} %param.13) | copy-start | bytes 1769476
  144.2 13.6 %all-to-all-start.6 = ((bf16[4,144,768]{2,1,0:T(8,128)(2,1)}), bf16[4,144,768]{2,1,0:T(8,128)(2,1)S(1)}, u32[]{:S(2)}, u32[]{:S(2)}) async-start(bf16[4,144,768]{2,1,0:T(8,128)(2,1)} %stack.3), calls=%async_computation.7 | async-start | bytes 1769472 | tf_op jit(solution)/shard_map/all_to_all | solution.py:122
  149.1 45.4 %reduce-scatter.2.cloned.1.call-start = ((), (), s32[]{:S(2)}) async-start(), calls=%async_computation.8 | async-start | bytes 884736 | tf_op jit(solution)/shard_map/reduce_scatter | solution.py:102
  150.3 2.1 %copy-start.2 = (bf16[1536,128]{1,0:T(8,128)(2,1)S(1)}, bf16[1536,128]{1,0:T(8,128)(2,1)}, u32[]{:S(2)}) copy-start(bf16[1536,128]{1,0:T(8,128)(2,1)} %param.15) | copy-start | bytes 1179652
  157.8 4.3 %collective-permute-start.2 = (bf16[576,768]{1,0:T(8,128)(2,1)S(1)}, bf16[576,768]{1,0:T(8,128)(2,1)S(1)}, u32[]{:S(2)}, u32[]{:S(2)}) collective-permute-start(bf16[576,768]{1,0:T(8,128)(2,1)S(1)} %bitcast.84), channel_id=1, source_target_pairs={{0,8},{8,0},{1,9},{9,1},{2,10},{10,2},{3,11},{11,3},{4,12},{12,4},... | collective-permute-start | bytes 2654216 | tf_op jit(solution)/shard_map/ppermute | solution.py:15
Sparse Core Ops, SparseCore 0:
  153.9 40.6 reduce-scatter.1
